TPU v7x, 128 devices: a whole 4x4x4 slice. The times are simulated.
128 devices in a mesh: req: 16 (over z, y), kv: 8 (over x, core).
Axes of the slice: x: 4, y: 4, z: 4, core: 2. Of those that a mesh axis runs over, the one named last changes fastest.
Arguments:
- hidden_in: bfloat16 [16384, 2048], P(('req', 'kv')), may hold values from -6 to 6
- slot_tokens: int32 [16384], replicated, may hold values from 0 to 16383, as said below
- cache_len: int32 [128], P('req'), may hold values from 1 to 2048, 65536 in all
- prefill_start: int32 [16], P('req'), may hold values from 0 to 2048
- key_cache: bfloat16 [128, 2048, 1024], P('req', None, 'kv')
- value_cache: bfloat16 [128, 2048, 1024], P('req', None, 'kv'), may hold values from -18 to 18
- key_prefix: bfloat16 [16, 2048, 1024], P('req', None, 'kv')
- value_prefix: bfloat16 [16, 2048, 1024], P('req', None, 'kv'), may hold values from -18 to 18
- attn_gain: float32 [2048], replicated, may hold values from 0.25 to 1.75
- q_proj: bfloat16 [2048, 2048], P(None, 'kv'), may hold values from -0.125 to 0.125
- k_proj: bfloat16 [2048, 1024], P(None, 'kv'), may hold values from -0.125 to 0.125
- v_proj: bfloat16 [2048, 1024], P(None, 'kv'), may hold values from -0.125 to 0.125
- q_gain: float32 [128], replicated, may hold values from 0.25 to 1.75
- k_gain: float32 [128], replicated, may hold values from 0.25 to 1.75
- o_proj: bfloat16 [2048, 2048], P('kv'), may hold values from -0.125 to 0.125
- ffn_gain: float32 [2048], replicated, may hold values from 0.25 to 1.75
- w_gate: bfloat16 [2048, 6144], P(None, 'req'), may hold values from -0.125 to 0.125
- w_up: bfloat16 [2048, 6144], P(None, 'req'), may hold values from -0.125 to 0.125
- w_down: bfloat16 [6144, 2048], P('req'), may hold values from -0.078125 to 0.078125
- final_gain: float32 [2048], replicated, may hold values from 0.25 to 1.75
- lm_head: bfloat16 [2048, 151936], P(None, ('req', 'kv')), may hold values from -0.375 to 0.375
Outputs:
- layer_out: bfloat16 [16384, 2048], P(('req', 'kv'))
- max_logit: float32 [144], replicated
Inputs may be any that keep to these rules, and one draw needn't show every extreme that they name: slot_tokens is a permutation of the batch's tokens; each device's 128 consecutive slots take exactly 1 token from each device's 128 consecutive batch tokens.
All inputs are finite; a program needn't handle non-finite values. No bound on the sum of `cache_len` on one device may be relied on, other than what follows from the above.
Results may differ from a plain program's by a relative error of at most 0.0085.
The roundings to bfloat16 on the way count: a program that leaves them out, or rounds other values in their place, can miss the bound.
Values may be sent and summed in bfloat16 or wider, within the bound.
A program may use at most 128 MiB of HBM per device.

v0:
```python
import jax
import jax.numpy as jnp
from jax import lax
from jax.sharding import PartitionSpec as P

EPS = 1e-06
NEG = -1e30


def spread(value, axis, root):
    mine = lax.axis_index(axis) == root
    return lax.psum(jnp.where(mine, value, jnp.zeros_like(value)), axis)


def norm_rows(values, gain_vec):
    wide = values.astype(jnp.float32)
    return wide * lax.rsqrt(jnp.mean(wide * wide, axis=-1, keepdims=True) + EPS) * gain_vec


def rotate(values, places):
    half_dim = values.shape[-1] // 2
    freqs = 1000000.0 ** (-(jnp.arange(half_dim, dtype=jnp.float32) * 2.0 / values.shape[-1]))
    angles = places[:, None] * freqs[None, :]
    cosine = jnp.cos(angles)[:, None, :]
    sine = jnp.sin(angles)[:, None, :]
    first_half = values[..., :half_dim]
    second_half = values[..., half_dim:]
    return jnp.concatenate(
        [first_half * cosine - second_half * sine, second_half * cosine + first_half * sine],
        axis=-1,
    )


def prefill_full(q_heads, key_old, value_old, key_new, value_new, start_at):
    old_len = key_old.shape[0]
    fresh_rows = q_heads.shape[0]
    factor = q_heads.shape[-1] ** (-0.5)
    all_keys = jnp.concatenate([key_old, key_new], axis=0)
    all_values = jnp.concatenate([value_old, value_new], axis=0)
    scores = (
        jnp.einsum("cgd,kd->gck", q_heads, all_keys, preferred_element_type=jnp.float32) * factor
    )
    key_index = jnp.arange(old_len + fresh_rows, dtype=jnp.int32)[None, :]
    row_index = jnp.arange(fresh_rows, dtype=jnp.int32)[:, None]
    allowed = jnp.where(key_index < old_len, key_index < start_at, key_index - old_len <= row_index)
    scores = jnp.where(allowed[None], scores, NEG)
    row_peak = jnp.max(scores, axis=-1, keepdims=True)
    expd = jnp.exp(scores - row_peak)
    weights = (expd / jnp.sum(expd, axis=-1, keepdims=True)).astype(jnp.bfloat16)
    return jnp.einsum(
        "gck,kd->cgd", weights, all_values, preferred_element_type=jnp.float32
    ).astype(jnp.bfloat16)


def decode_attend(q_heads, key_old, value_old, key_self, value_self, lengths):
    factor = q_heads.shape[-1] ** (-0.5)
    past = jnp.einsum("bgd,bld->bgl", q_heads, key_old, preferred_element_type=jnp.float32) * factor
    slot_index = jnp.arange(key_old.shape[1], dtype=jnp.int32)
    past = jnp.where(slot_index[None, None, :] < lengths[:, None, None], past, NEG)
    own_score = (
        jnp.einsum("bgd,bd->bg", q_heads, key_self, preferred_element_type=jnp.float32) * factor
    )
    row_peak = jnp.maximum(jnp.max(past, axis=-1), own_score)
    past_exp = jnp.exp(past - row_peak[..., None])
    own_exp = jnp.exp(own_score - row_peak)
    row_total = jnp.sum(past_exp, axis=-1) + own_exp
    past_w = (past_exp / row_total[..., None]).astype(jnp.bfloat16)
    own_w = (own_exp / row_total).astype(jnp.bfloat16)
    summed = jnp.einsum("bgl,bld->bgd", past_w, value_old, preferred_element_type=jnp.float32)
    summed = (
        summed + own_w.astype(jnp.float32)[..., None] * value_self.astype(jnp.float32)[:, None, :]
    )
    return summed.astype(jnp.bfloat16)


def regroup(rows_in):
    return lax.all_to_all(rows_in, ("req", "kv"), split_axis=0, concat_axis=0, tiled=True)


def shards(
    hidden_in,
    slot_tokens,
    cache_len,
    prefill_start,
    key_cache,
    value_cache,
    key_prefix,
    value_prefix,
    attn_gain,
    q_proj,
    k_proj,
    v_proj,
    q_gain,
    k_gain,
    o_proj,
    ffn_gain,
    w_gate,
    w_up,
    w_down,
    final_gain,
    lm_head,
):
    req_count = lax.axis_size("req")
    kv_count = lax.axis_size("kv")
    devices = req_count * kv_count
    rows_dev = hidden_in.shape[0]
    per_pair = rows_dev // devices
    self_index = lax.axis_index("req") * kv_count + lax.axis_index("kv")
    slot_table = slot_tokens.reshape(devices, rows_dev)
    from_self = slot_table // rows_dev == self_index
    picked = jnp.argsort(jnp.where(from_self, 0, 1).astype(jnp.int32), axis=1, stable=True)[
        :, :per_pair
    ]
    send_rows = (jnp.take_along_axis(slot_table, picked, axis=1) - self_index * rows_dev).reshape(
        -1
    )
    own_sources = lax.dynamic_index_in_dim(slot_table, self_index, 0, keepdims=False) // rows_dev
    marks = (own_sources[:, None] == jnp.arange(devices, dtype=jnp.int32)[None, :]).astype(
        jnp.int32
    )
    ranks = jnp.sum(marks * (jnp.cumsum(marks, axis=0) - 1), axis=1)
    slot_place = own_sources * per_pair + ranks
    arrived = regroup(hidden_in[send_rows])
    owner_rows = arrived[slot_place]
    normed = norm_rows(owner_rows, attn_gain).astype(jnp.bfloat16)
    q_cols = q_proj.shape[1]
    kv_cols = k_proj.shape[1]
    rows_piece = lax.all_gather(normed, "kv", axis=0, tiled=True)
    projected = jnp.concatenate(
        [
            jnp.dot(rows_piece, q_proj, preferred_element_type=jnp.float32),
            jnp.dot(rows_piece, k_proj, preferred_element_type=jnp.float32),
            jnp.dot(rows_piece, v_proj, preferred_element_type=jnp.float32),
        ],
        axis=1,
    )
    tok_req = projected.shape[0]
    head_dim = q_gain.shape[0]
    dec_count = cache_len.shape[0]
    fresh_count = tok_req - dec_count
    q_raw = projected[:, :q_cols].reshape(tok_req, q_cols // head_dim, head_dim)
    k_raw = projected[:, q_cols : q_cols + kv_cols].reshape(tok_req, kv_cols // head_dim, head_dim)
    v_new = (
        projected[:, q_cols + kv_cols :]
        .astype(jnp.bfloat16)
        .reshape(tok_req, kv_cols // head_dim, head_dim)
    )
    places = jnp.concatenate(
        [prefill_start[0] + jnp.arange(fresh_count, dtype=jnp.int32), cache_len]
    ).astype(jnp.float32)
    queries = rotate(norm_rows(q_raw, q_gain), places).astype(jnp.bfloat16)
    keys_new = rotate(norm_rows(k_raw, k_gain), places).astype(jnp.bfloat16)
    pre_out = prefill_full(
        queries[:fresh_count],
        key_prefix[0, :, 0:head_dim],
        value_prefix[0, :, 0:head_dim],
        keys_new[:fresh_count, 0],
        v_new[:fresh_count, 0],
        prefill_start[0],
    )
    dec_out = decode_attend(
        queries[fresh_count:],
        key_cache,
        value_cache,
        keys_new[fresh_count:, 0],
        v_new[fresh_count:, 0],
        cache_len,
    )
    pieces = jnp.concatenate([pre_out, dec_out], axis=0)
    attended = pieces.reshape(tok_req, q_cols)
    attn_part = lax.psum_scatter(
        jnp.dot(attended, o_proj, preferred_element_type=jnp.float32),
        "kv",
        scatter_dimension=0,
        tiled=True,
    )
    resid = (owner_rows.astype(jnp.float32) + attn_part).astype(jnp.bfloat16)
    ffn_in = norm_rows(resid, ffn_gain).astype(jnp.bfloat16)
    rows_piece = lax.all_gather(ffn_in, "req", axis=0, tiled=True)
    gate_part = jnp.dot(rows_piece, w_gate, preferred_element_type=jnp.float32)
    up_part = jnp.dot(rows_piece, w_up, preferred_element_type=jnp.float32)
    hidden_act = (jax.nn.silu(gate_part) * up_part).astype(jnp.bfloat16)
    ffn_part = lax.psum_scatter(
        jnp.dot(hidden_act, w_down, preferred_element_type=jnp.float32),
        "req",
        scatter_dimension=0,
        tiled=True,
    )
    out_rows = (resid.astype(jnp.float32) + ffn_part).astype(jnp.bfloat16)
    going_back = jnp.zeros_like(out_rows).at[slot_place].set(out_rows)
    returned = regroup(going_back)
    layer_out = jnp.zeros_like(hidden_in).at[send_rows].set(returned)
    tail_rows = norm_rows(out_rows[rows_dev - dec_count - 1 :], final_gain).astype(jnp.bfloat16)
    tail_rows = spread(tail_rows, "kv", kv_count - 1)
    local_peaks = jnp.max(
        jnp.dot(
            lax.all_gather(tail_rows, "req", axis=0, tiled=True),
            lm_head,
            preferred_element_type=jnp.float32,
        ),
        axis=1,
    )
    max_logit = lax.pmax(local_peaks, ("req", "kv"))
    return (layer_out, max_logit)


def solution(mesh):
    placed = (
        P(("req", "kv"), None),
        P(),
        P("req"),
        P("req"),
        P("req", None, "kv"),
        P("req", None, "kv"),
        P("req", None, "kv"),
        P("req", None, "kv"),
        P(),
        P(None, "kv"),
        P(None, "kv"),
        P(None, "kv"),
        P(),
        P(),
        P("kv", None),
        P(),
        P(None, "req"),
        P(None, "req"),
        P("req", None),
        P(),
        P(None, ("req", "kv")),
    )
    return jax.shard_map(
        shards, mesh=mesh, in_specs=placed, out_specs=(P(("req", "kv"), None), P()), check_vma=False
    )
```

profile of v0, /device:TPU:1, one launch (start us, length us, event | category | flops | bytes accessed | tf_op | source)
XLA Modules:
  0.0 540.3 jit_solution(2482450521483599496)
XLA Ops:
  11.1 4.7 sort.19.cloned.1.call-done
  17.0 1.9 gather_fusion.2
  23.6 11.5 %all-to-all-start = ((bf16[128,2,1024]{2,1,0:T(2,128)(2,1)}), bf16[128,2,1024]{2,1,0:T(2,128)(2,1)S(1)}, u32[]{:S(2)}, u32[]{:S(2)}) async-start(bf16[128,2,1024]{2,1,0:T(2,128)(2,1)} %reshape.484), calls=%async_computation | async-start | bytes 1048576 | tf_op jit(solution)/shard_map/all_to_all | solution.py:77
  35.9 13.0 %all-to-all-done = bf16[128,2,1024]{2,1,0:T(2,128)(2,1)S(1)} async-done(((bf16[128,2,1024]{2,1,0:T(2,128)(2,1)}), bf16[128,2,1024]{2,1,0:T(2,128)(2,1)S(1)}, u32[]{:S(2)}, u32[]{:S(2)}) %all-to-all-start) | async-done | bytes 524320 | tf_op jit(solution)/shard_map/all_to_all | solution.py:77
  55.4 3.1 multiply_cosine_fusion
  58.6 4.2 fusion.4
  62.7 20.4 %all-gather.4.cloned.1.call-done = bf16[1024,2048]{1,0:T(8,128)(2,1)} async-done(((bf16[128,2048]{1,0:T(8,128)(2,1)}), bf16[1024,2048]{1,0:T(8,128)(2,1)}) %all-gather.4.cloned.1.call-update) | async-done | bytes 4194320 | tf_op jit(solution)/shard_map/all_gather | solution.py:128
  83.2 3.6 convolution_convert_fusion
  90.5 2.3 multiply_reduce_fusion
  99.4 2.9 fusion.43
  102.4 15.9 %fusion.84 = (f32[2,1016]{1,0:T(2,128)S(1)}, f32[2,1016,3064]{2,1,0:T(8,128)}) fusion(pred[1016,3064]{1,0:T(8,128)(4,1)} %fusion.4, bf16[1016,128]{1,0:T(8,128)(2,1)} %copy.80, bf16[2048,128]{1,0:T(8,128)(2,1)} %bitcast.105, bf16[1024,2,64]{2,0,1:T(8,128)(2,1)S(1)} %get-tuple-element.6, bf16[1024,2,64]{2,0,1:T(8,128)(2,1)S(1)} %get-tuple-element.7), kind=kOutput, calls=%fused_computation.161 | convolution fusion | flops 1621384704 | bytes 29334016 | tf_op jit(solution)/shard_map/sub | solution.py:48
  118.3 11.7 %fusion.12 = bf16[1016,2,128]{2,0,1:T(8,128)(2,1)S(1)} fusion(f32[2,1016,3064]{2,1,0:T(8,128)} %get-tuple-element.21, f32[2,1016]{1,0:T(2,128)S(1)} %get-tuple-element.20, bf16[1016,128]{1,0:T(8,128)(2,1)S(1)} %copy-done.5, bf16[2048,128]{1,0:T(8,128)(2,1)} %bitcast.106), kind=kOutput, calls=%fused_computation.28 | convolution fusion | flops 1608149248 | bytes 26216896 | tf_op jit(solution)/shard_map/gck,kd->cgd/dot_general | solution.py:50
  130.3 5.7 %fusion.89 = f32[1024,2048]{1,0:T(8,128)} fusion(bf16[1024,256]{0,1:T(8,128)(2,1)S(1)} %bitcast.94, bf16[256,2048]{1,0:T(8,128)(2,1)} %param.35), kind=kOutput, calls=%fused_computation.162 | convolution fusion | flops 1073741824 | bytes 9961472 | tf_op jit(solution)/shard_map/dot_general | solution.py:172
  136.1 51.5 %reduce-scatter.3.cloned.1.call-done = f32[128,2048]{1,0:T(8,128)} async-done(((f32[1024,2048]{1,0:T(8,128)}), f32[128,2048]{1,0:T(8,128)}) %reduce-scatter.3.cloned.1.call-update) | async-done | bytes 1048592 | tf_op jit(solution)/shard_map/reduce_scatter | solution.py:171
  190.4 71.2 %all-gather.6.cloned.1.call-done = bf16[2048,2048]{1,0:T(8,128)(2,1)} async-done(((bf16[128,2048]{1,0:T(8,128)(2,1)}), bf16[2048,2048]{1,0:T(8,128)(2,1)}) %all-gather.6.cloned.1.call-update) | async-done | bytes 8388624 | tf_op jit(solution)/shard_map/all_gather | solution.py:179
  261.5 10.1 %fusion.90 = f32[2048,384]{1,0:T(8,128)} fusion(bf16[2048,2048]{1,0:T(8,128)(2,1)} %all-gather.6.cloned.1.call-done, bf16[2048,384]{1,0:T(8,128)(2,1)} %param.37), kind=kOutput, calls=%fused_computation.163 | convolution fusion | flops 3221225472 | bytes 13107200 | tf_op jit(solution)/shard_map/dot_general | solution.py:180
  271.6 15.4 %fusion.10 = f32[2048,2048]{1,0:T(8,128)} fusion(bf16[384,2048]{1,0:T(8,128)(2,1)S(1)} %copy-done, f32[2048,384]{1,0:T(8,128)} %fusion.90, bf16[2048,2048]{1,0:T(8,128)(2,1)} %all-gather.6.cloned.1.call-done, bf16[2048,384]{1,0:T(8,128)(2,1)} %param.38), kind=kOutput, calls=%fused_computation.26 | convolution fusion | flops 6447169536 | bytes 31457280 | tf_op jit(solution)/shard_map/dot_general | solution.py:184
  287.0 110.1 %reduce-scatter.5.cloned.1.call-done = f32[128,2048]{1,0:T(8,128)} async-done(((f32[2048,2048]{1,0:T(8,128)}), f32[128,2048]{1,0:T(8,128)}) %reduce-scatter.5.cloned.1.call-update) | async-done | bytes 1048592 | tf_op jit(solution)/shard_map/reduce_scatter | solution.py:183
  402.4 23.1 %psum.7 = bf16[9,2048]{1,0:T(8,128)(2,1)S(1)} all-reduce(bf16[9,2048]{1,0:T(8,128)(2,1)S(1)} %fusion.48), channel_id=1, replica_groups=mesh['req'=16,'kv'=8] {'kv'}, use_global_device_ids=true, to_apply=%region_16.17 | all-reduce | flops 18432 | bytes 73728 | tf_op jit(solution)/shard_map/psum | solution.py:12
  425.5 8.6 %all-to-all-start.1 = ((bf16[128,2,1024]{2,1,0:T(2,128)(2,1)}), bf16[128,2,1024]{2,1,0:T(2,128)(2,1)S(1)}, u32[]{:S(2)}, u32[]{:S(2)}) async-start(bf16[128,2,1024]{2,1,0:T(2,128)(2,1)} %reshape.486), calls=%async_computation.3 | async-start | bytes 1048576 | tf_op jit(solution)/shard_map/all_to_all | solution.py:77
  434.1 22.4 %all-gather = bf16[16,9,2048]{2,1,0:T(8,128)(2,1)S(1)} all-gather(bf16[1,9,2048]{2,1,0:T(8,128)(2,1)S(1)} %bitcast.99), channel_id=1, replica_groups=mesh['req'=16,'kv'=8] {'req'}, dimensions={0}, use_global_device_ids=true | all-gather | bytes 626688 | tf_op jit(solution)/shard_map/all_gather | solution.py:197
  457.5 4.4 convolution_reduce_fusion
  461.9 68.8 %pmax.7 = f32[144]{0:T(256)} all-reduce(f32[144]{0:T(256)S(1)} %convolution_reduce_fusion), channel_id=1, replica_groups=mesh['req'=16,'kv'=8] {'req','kv'}, use_global_device_ids=true, to_apply=%region_18.19 | all-reduce | flops 144 | bytes 1152 | tf_op jit(solution)/shard_map/pmax | solution.py:203
  531.1 2.4 scatter_custom_fusion.1
  (110 shorter events, 36.5 us)
Async XLA Ops:
  7.2 264.4 %copy-start = (bf16[384,2048]{1,0:T(8,128)(2,1)S(1)}, bf16[384,2048]{1,0:T(8,128)(2,1)}, u32[]{:S(2)}) copy-start(bf16[384,2048]{1,0:T(8,128)(2,1)} %param.39) | copy-start | bytes 4718596
  7.2 12.8 %copy-start.1 = (bf16[128,2048]{1,0:T(8,128)(2,1)S(1)}, bf16[128,2048]{1,0:T(8,128)(2,1)}, u32[]{:S(2)}) copy-start(bf16[128,2048]{1,0:T(8,128)(2,1)} %param.21) | copy-start | bytes 1572868
  7.2 8.5 %sort.19.cloned.1.call-start = ((), (), s32[]{:S(2)}) async-start(), calls=%async_computation.8 | async-start | bytes 393248 | tf_op jit(solution)/shard_map/jit(argsort)/sort | solution.py:111
  23.6 25.2 %all-to-all-start = ((bf16[128,2,1024]{2,1,0:T(2,128)(2,1)}), bf16[128,2,1024]{2,1,0:T(2,128)(2,1)S(1)}, u32[]{:S(2)}, u32[]{:S(2)}) async-start(bf16[128,2,1024]{2,1,0:T(2,128)(2,1)} %reshape.484), calls=%async_computation | async-start | bytes 1048576 | tf_op jit(solution)/shard_map/all_to_all | solution.py:77
  35.1 48.0 %all-gather.4.cloned.1.call-start = ((), (), s32[]{:S(2)}) async-start(), calls=%async_computation.4 | async-start | bytes 4718592 | tf_op jit(solution)/shard_map/all_gather | solution.py:128
  35.9 17.4 %copy-start.6 = (f32[2048]{0:T(1024)S(1)}, f32[2048]{0:T(1024)}, u32[]{:S(2)}) copy-start(f32[2048]{0:T(1024)} %param.29) | copy-start | bytes 24580
  50.6 4.7 copy-start.9
  53.1 30.1 %copy-start.13 = (bf16[2048,128]{1,0:T(8,128)(2,1)S(1)}, bf16[2048,128]{1,0:T(8,128)(2,1)}, u32[]{:S(2)}) copy-start(bf16[2048,128]{1,0:T(8,128)(2,1)} %param.32) | copy-start | bytes 1572868
  54.3 133.4 %reduce-scatter.3.cloned.1.call-start = ((), (), s32[]{:S(2)}) async-start(), calls=%async_computation.5 | async-start | bytes 9437184 | tf_op jit(solution)/shard_map/reduce_scatter | solution.py:171
  62.7 24.8 %copy-start.4 = (bf16[2048,128]{1,0:T(8,128)(2,1)S(1)}, bf16[2048,128]{1,0:T(8,128)(2,1)}, u32[]{:S(2)}) copy-start(bf16[2048,128]{1,0:T(8,128)(2,1)} %param.31) | copy-start | bytes 1572868
  83.2 4.4 copy-start.3
  86.8 2.3 copy-start.10
  86.8 3.7 copy-start.12
  90.5 4.8 copy-start.11
  95.3 2.5 copy-start.2
  102.4 15.9 %copy-start.5 = (bf16[1016,128]{1,0:T(8,128)(2,1)S(1)}, bf16[1016,128]{1,0:T(8,128)(2,1)}, u32[]{:S(2)}) copy-start(bf16[1016,128]{1,0:T(8,128)(2,1)} %slice.58) | copy-start | bytes 780292
  136.1 53.1 %copy-start.7 = (f32[2048]{0:T(1024)S(1)}, f32[2048]{0:T(1024)}, u32[]{:S(2)}) copy-start(f32[2048]{0:T(1024)} %param.36) | copy-start | bytes 24580
  136.1 125.4 %all-gather.6.cloned.1.call-start = ((), (), s32[]{:S(2)}) async-start(), calls=%async_computation.6 | async-start | bytes 8912896 | tf_op jit(solution)/shard_map/all_gather | solution.py:179
  190.1 207.0 %reduce-scatter.5.cloned.1.call-start = ((), (), s32[]{:S(2)}) async-start(), calls=%async_computation.7 | async-start | bytes 17825792 | tf_op jit(solution)/shard_map/reduce_scatter | solution.py:183
  287.0 115.3 %copy-start.8 = (f32[2048]{0:T(1024)S(1)}, f32[2048]{0:T(1024)}, u32[]{:S(2)}) copy-start(f32[2048]{0:T(1024)} %param.40) | copy-start | bytes 24580
  425.5 105.2 %all-to-all-start.1 = ((bf16[128,2,1024]{2,1,0:T(2,128)(2,1)}), bf16[128,2,1024]{2,1,0:T(2,128)(2,1)S(1)}, u32[]{:S(2)}, u32[]{:S(2)}) async-start(bf16[128,2,1024]{2,1,0:T(2,128)(2,1)} %reshape.486), calls=%async_computation.3 | async-start | bytes 1048576 | tf_op jit(solution)/shard_map/all_to_all | solution.py:77
Sparse Core Ops, SparseCore 0:
  10.8 4.6 sort.21.cloned.1.call-done
  54.4 28.7 all-gather.3
  136.2 51.3 reduce-scatter.2
  190.4 71.0 all-gather.5
  287.1 109.9 reduce-scatter.4
  (1 shorter events, 0.0 us)
where the time goes:
time: 545 us; the launch traced here: 540 us
  waiting for transfers between devices  266 us (49%)
  blocking collectives  114 us (21%)
  matrix products  74.9 us (14%)
  local copies, waits for them, and re-layouts  25.5 us (5%)
  other arithmetic  23.6 us (4%)
  starting transfers between devices  20.7 us (4%)
  between operations  15 us (3%)
    reduce_scatter x1, waiting for transfers between devices, shards(): lax.psum_scatter(jnp.dot(hidden_act, w_down, preferred_element_type=jnp.f...  110 us
    all_gather x1, waiting for transfers between devices, shards(): rows_piece = lax.all_gather(ffn_in, 'req', axis=0, tiled=True)  71.2 us
    pmax x1, blocking collectives, shards(): max_logit = lax.pmax(local_peaks, ('req', 'kv'))  68.8 us
    reduce_scatter x1, waiting for transfers between devices, shards(): lax.psum_scatter(jnp.dot(attended, o_proj, preferred_element_type=jnp.flo...  51.5 us
    psum x1, blocking collectives, spread(): return lax.psum(jnp.where(mine, value, jnp.zeros_like(value)), axis)  23.1 us
    all_gather x1, blocking collectives, shards(): lax.all_gather(tail_rows, 'req', axis=0, tiled=True)  22.4 us
    all_gather x1, waiting for transfers between devices, shards(): rows_piece = lax.all_gather(normed, 'kv', axis=0, tiled=True)  20.4 us
    all_to_all x2, starting transfers between devices, regroup(): lax.all_to_all(rows_in, ('req', 'kv'), split_axis=0, concat_axis=0, tiled...  20.1 us
  transfers between devices with their start and end apart: 6, of which 5 were waited for; matrix products, arithmetic and copies ran while one was open for 3% of the time, Pallas kernels for 0%

commit v1 on v0

--- a/solution.py
+++ b/solution.py
@@ -5,6 +5,24 @@
 
 EPS = 1e-06
 NEG = -1e30
+
+
+def ring_gather(shard, axis, dim):
+    ways, here, turn = (lax.axis_size(axis), lax.axis_index(axis), shard.shape[dim])
+    dims = [n * ways if d == dim else n for d, n in enumerate(shard.shape)]
+    full = lax.dynamic_update_slice_in_dim(
+        jnp.zeros(dims, shard.dtype), shard, here * turn, axis=dim
+    )
+    going_up = going_down = shard
+    for far in range(1, ways // 2 + 1):
+        going_up = lax.ppermute(going_up, axis, [(d, (d + 1) % ways) for d in range(ways)])
+        full = lax.dynamic_update_slice_in_dim(full, going_up, (here - far) % ways * turn, axis=dim)
+        if 2 * far < ways:
+            going_down = lax.ppermute(going_down, axis, [(d, (d - 1) % ways) for d in range(ways)])
+            full = lax.dynamic_update_slice_in_dim(
+                full, going_down, (here + far) % ways * turn, axis=dim
+            )
+    return full
 
 
 def spread(value, axis, root):
@@ -193,11 +211,7 @@
     tail_rows = norm_rows(out_rows[rows_dev - dec_count - 1 :], final_gain).astype(jnp.bfloat16)
     tail_rows = spread(tail_rows, "kv", kv_count - 1)
     local_peaks = jnp.max(
-        jnp.dot(
-            lax.all_gather(tail_rows, "req", axis=0, tiled=True),
-            lm_head,
-            preferred_element_type=jnp.float32,
-        ),
+        jnp.dot(ring_gather(tail_rows, "req", 0), lm_head, preferred_element_type=jnp.float32),
         axis=1,
     )
     max_logit = lax.pmax(local_peaks, ("req", "kv"))

time: 545 us -> 586 us (1.075)
  starting transfers between devices: 20.7 us -> 62.2 us
  blocking collectives: 114 us -> 89.5 us
  local copies, waits for them, and re-layouts: 25.5 us -> 38.2 us
  waiting for transfers between devices: 266 us -> 277 us
    ppermute x0 -> x15, starting transfers between devices: none -> 35.7 us  [the longest x7 34.1 us: ring_gather(): lax.ppermute(going_down, axis, [(d, (d - 1) % ways) for d in range(ways)])]
    all_gather x1 -> x0, blocking collectives: 22.4 us -> none  [shards(): lax.all_gather(tail_rows, 'req', axis=0, tiled=True)]
    dynamic_update_slice x0 -> x16, local copies, waits for them, and re-layouts: none -> 12.1 us  [the longest x8 5.9 us: ring_gather(): lax.dynamic_update_slice_in_dim(full, going_up, (here - far) % ways * tur...]
    ppermute x0 -> x15, waiting for transfers between devices: none -> 11.6 us  [the longest x8 7.6 us: ring_gather(): lax.ppermute(going_up, axis, [(d, (d + 1) % ways) for d in range(ways)])]
  transfers between devices with their start and end apart: 6 -> 21, of which waited for: 5 -> 13; matrix products, arithmetic and copies ran while one was open for 3% -> 5% of each run, Pallas kernels for 0% -> 0%
where the time goes in v1:
time: 586 us; the launch traced here: 581 us
  waiting for transfers between devices  277 us (47%)
  blocking collectives  89.5 us (15%)
  matrix products  74.7 us (13%)
  starting transfers between devices  62.2 us (11%)
  local copies, waits for them, and re-layouts  38.2 us (7%)
  other arithmetic  24.1 us (4%)
  between operations  15.2 us (3%)
    reduce_scatter x1, waiting for transfers between devices, shards(): lax.psum_scatter(jnp.dot(hidden_act, w_down, preferred_element_type=jnp.f...  110 us
    all_gather x1, waiting for transfers between devices, shards(): rows_piece = lax.all_gather(ffn_in, 'req', axis=0, tiled=True)  71.2 us
    pmax x1, blocking collectives, shards(): max_logit = lax.pmax(local_peaks, ('req', 'kv'))  66.4 us
    reduce_scatter x1, waiting for transfers between devices, shards(): lax.psum_scatter(jnp.dot(attended, o_proj, preferred_element_type=jnp.flo...  51.5 us
    ppermute x7, starting transfers between devices, ring_gather(): lax.ppermute(going_down, axis, [(d, (d - 1) % ways) for d in range(ways)])  34.1 us
    all_to_all x2, starting transfers between devices, regroup(): lax.all_to_all(rows_in, ('req', 'kv'), split_axis=0, concat_axis=0, tiled...  25.8 us
    psum x1, blocking collectives, spread(): return lax.psum(jnp.where(mine, value, jnp.zeros_like(value)), axis)  23.1 us
    all_gather x1, waiting for transfers between devices, shards(): rows_piece = lax.all_gather(normed, 'kv', axis=0, tiled=True)  20.4 us
  transfers between devices with their start and end apart: 21, of which 13 were waited for; matrix products, arithmetic and copies ran while one was open for 5% of the time, Pallas kernels for 0%

profile of v1, /device:TPU:1, one launch (start us, length us, event | category | flops | bytes accessed | tf_op | source)
XLA Modules:
  0.0 580.9 jit_solution(13785249885975179417)
XLA Ops:
  10.3 5.5 sort.19.cloned.1.call-done
  24.0 11.5 %all-to-all-start = ((bf16[128,2,1024]{2,1,0:T(2,128)(2,1)}), bf16[128,2,1024]{2,1,0:T(2,128)(2,1)S(1)}, u32[]{:S(2)}, u32[]{:S(2)}) async-start(bf16[128,2,1024]{2,1,0:T(2,128)(2,1)} %reshape.482), calls=%async_computation | async-start | bytes 1048576 | tf_op jit(solution)/shard_map/all_to_all | solution.py:95
  37.1 12.1 %all-to-all-done = bf16[128,2,1024]{2,1,0:T(2,128)(2,1)S(1)} async-done(((bf16[128,2,1024]{2,1,0:T(2,128)(2,1)}), bf16[128,2,1024]{2,1,0:T(2,128)(2,1)S(1)}, u32[]{:S(2)}, u32[]{:S(2)}) %all-to-all-start) | async-done | bytes 524320 | tf_op jit(solution)/shard_map/all_to_all | solution.py:95
  59.0 4.2 fusion.4
  63.2 20.4 %all-gather.3.cloned.1.call-done = bf16[1024,2048]{1,0:T(8,128)(2,1)} async-done(((bf16[128,2048]{1,0:T(8,128)(2,1)}), bf16[1024,2048]{1,0:T(8,128)(2,1)}) %all-gather.3.cloned.1.call-update) | async-done | bytes 4194320 | tf_op jit(solution)/shard_map/all_gather | solution.py:146
  83.6 3.9 multiply_reduce_fusion.1
  103.3 15.9 %fusion.84 = (f32[2,1016]{1,0:T(2,128)S(1)}, f32[2,1016,3064]{2,1,0:T(8,128)}) fusion(pred[1016,3064]{1,0:T(8,128)(4,1)} %fusion.4, bf16[1016,128]{1,0:T(8,128)(2,1)} %copy.80, bf16[2048,128]{1,0:T(8,128)(2,1)} %bitcast.101, bf16[1024,2,64]{2,0,1:T(8,128)(2,1)S(1)} %get-tuple-element.6, bf16[1024,2,64]{2,0,1:T(8,128)(2,1)S(1)} %get-tuple-element.7), kind=kOutput, calls=%fused_computation.161 | convolution fusion | flops 1621384704 | bytes 29334016 | tf_op jit(solution)/shard_map/sub | solution.py:66
  119.2 11.7 %fusion.12 = bf16[1016,2,128]{2,0,1:T(8,128)(2,1)S(1)} fusion(f32[2,1016,3064]{2,1,0:T(8,128)} %get-tuple-element.21, f32[2,1016]{1,0:T(2,128)S(1)} %get-tuple-element.20, bf16[1016,128]{1,0:T(8,128)(2,1)S(1)} %slice-done, bf16[2048,128]{1,0:T(8,128)(2,1)} %bitcast.102), kind=kOutput, calls=%fused_computation.28 | convolution fusion | flops 1608149248 | bytes 26216896 | tf_op jit(solution)/shard_map/gck,kd->cgd/dot_general | solution.py:68
  131.2 5.7 fusion.89
  137.0 51.5 %reduce-scatter.3.cloned.1.call-done = f32[128,2048]{1,0:T(8,128)} async-done(((f32[1024,2048]{1,0:T(8,128)}), f32[128,2048]{1,0:T(8,128)}) %reduce-scatter.3.cloned.1.call-update) | async-done | bytes 1048592 | tf_op jit(solution)/shard_map/reduce_scatter | solution.py:189
  191.2 71.2 %all-gather.5.cloned.1.call-done = bf16[2048,2048]{1,0:T(8,128)(2,1)} async-done(((bf16[128,2048]{1,0:T(8,128)(2,1)}), bf16[2048,2048]{1,0:T(8,128)(2,1)}) %all-gather.5.cloned.1.call-update) | async-done | bytes 8388624 | tf_op jit(solution)/shard_map/all_gather | solution.py:197
  262.4 10.1 %fusion.90 = f32[2048,384]{1,0:T(8,128)} fusion(bf16[2048,2048]{1,0:T(8,128)(2,1)} %all-gather.5.cloned.1.call-done, bf16[2048,384]{1,0:T(8,128)(2,1)} %param.37), kind=kOutput, calls=%fused_computation.163 | convolution fusion | flops 3221225472 | bytes 13107200 | tf_op jit(solution)/shard_map/dot_general | solution.py:198
  272.5 15.4 %fusion.10 = f32[2048,2048]{1,0:T(8,128)} fusion(bf16[384,2048]{1,0:T(8,128)(2,1)S(1)} %copy-done, f32[2048,384]{1,0:T(8,128)} %fusion.90, bf16[2048,2048]{1,0:T(8,128)(2,1)} %all-gather.5.cloned.1.call-done, bf16[2048,384]{1,0:T(8,128)(2,1)} %param.38), kind=kOutput, calls=%fused_computation.26 | convolution fusion | flops 6447169536 | bytes 31457280 | tf_op jit(solution)/shard_map/dot_general | solution.py:202
  287.9 110.1 %reduce-scatter.5.cloned.1.call-done = f32[128,2048]{1,0:T(8,128)} async-done(((f32[2048,2048]{1,0:T(8,128)}), f32[128,2048]{1,0:T(8,128)}) %reduce-scatter.5.cloned.1.call-update) | async-done | bytes 1048592 | tf_op jit(solution)/shard_map/reduce_scatter | solution.py:201
  399.6 23.1 %psum.7 = bf16[9,2048]{1,0:T(8,128)(2,1)S(1)} all-reduce(bf16[9,2048]{1,0:T(8,128)(2,1)S(1)} %fusion.48), channel_id=1, replica_groups=mesh['req'=16,'kv'=8] {'kv'}, use_global_device_ids=true, to_apply=%region_16.17 | all-reduce | flops 18432 | bytes 73728 | tf_op jit(solution)/shard_map/psum | solution.py:30
  429.2 4.8 collective-permute-start.3
  435.6 4.8 collective-permute-start.5
  442.1 4.9 collective-permute-start.7
  453.1 14.3 %all-to-all-start.1 = ((bf16[128,2,1024]{2,1,0:T(2,128)(2,1)}), bf16[128,2,1024]{2,1,0:T(2,128)(2,1)S(1)}, u32[]{:S(2)}, u32[]{:S(2)}) async-start(bf16[128,2,1024]{2,1,0:T(2,128)(2,1)} %reshape.484), calls=%async_computation.3 | async-start | bytes 1048576 | tf_op jit(solution)/shard_map/all_to_all | solution.py:95
  467.5 5.6 collective-permute-start.9
  476.0 5.6 collective-permute-start.11
  483.0 5.1 collective-permute-start.13
  500.6 4.2 convolution_reduce_fusion
  504.8 66.4 %pmax.7 = f32[144]{0:T(256)} all-reduce(f32[144]{0:T(256)S(1)} %convolution_reduce_fusion), channel_id=1, replica_groups=mesh['req'=16,'kv'=8] {'req','kv'}, use_global_device_ids=true, to_apply=%region_18.19 | all-reduce | flops 144 | bytes 1152 | tf_op jit(solution)/shard_map/pmax | solution.py:217
  (164 shorter events, 77.7 us)
Async XLA Ops:
  7.2 265.3 %copy-start = (bf16[384,2048]{1,0:T(8,128)(2,1)S(1)}, bf16[384,2048]{1,0:T(8,128)(2,1)}, u32[]{:S(2)}) copy-start(bf16[384,2048]{1,0:T(8,128)(2,1)} %param.39) | copy-start | bytes 4718596
  24.0 25.2 %all-to-all-start = ((bf16[128,2,1024]{2,1,0:T(2,128)(2,1)}), bf16[128,2,1024]{2,1,0:T(2,128)(2,1)S(1)}, u32[]{:S(2)}, u32[]{:S(2)}) async-start(bf16[128,2,1024]{2,1,0:T(2,128)(2,1)} %reshape.482), calls=%async_computation | async-start | bytes 1048576 | tf_op jit(solution)/shard_map/all_to_all | solution.py:95
  35.5 48.0 %all-gather.3.cloned.1.call-start = ((), (), s32[]{:S(2)}) async-start(), calls=%async_computation.4 | async-start | bytes 4718592 | tf_op jit(solution)/shard_map/all_gather | solution.py:146
  54.7 133.8 %reduce-scatter.3.cloned.1.call-start = ((), (), s32[]{:S(2)}) async-start(), calls=%async_computation.5 | async-start | bytes 9437184 | tf_op jit(solution)/shard_map/reduce_scatter | solution.py:189
  136.9 53.1 %copy-start.8 = (f32[2048]{0:T(1024)S(1)}, f32[2048]{0:T(1024)}, u32[]{:S(2)}) copy-start(f32[2048]{0:T(1024)} %param.36) | copy-start | bytes 24580
  137.0 125.4 %all-gather.5.cloned.1.call-start = ((), (), s32[]{:S(2)}) async-start(), calls=%async_computation.6 | async-start | bytes 8912896 | tf_op jit(solution)/shard_map/all_gather | solution.py:197
  191.0 207.0 %reduce-scatter.5.cloned.1.call-start = ((), (), s32[]{:S(2)}) async-start(), calls=%async_computation.7 | async-start | bytes 17825792 | tf_op jit(solution)/shard_map/reduce_scatter | solution.py:201
  287.9 111.6 %copy-start.9 = (f32[2048]{0:T(1024)S(1)}, f32[2048]{0:T(1024)}, u32[]{:S(2)}) copy-start(f32[2048]{0:T(1024)} %param.40) | copy-start | bytes 24580
  422.7 6.5 %collective-permute-start = (bf16[9,2048]{1,0:T(8,128)(2,1)S(1)}, bf16[9,2048]{1,0:T(8,128)(2,1)S(1)}, u32[]{:S(2)}, u32[]{:S(2)}) collective-permute-start(bf16[9,2048]{1,0:T(8,128)(2,1)S(1)} %psum.7), channel_id=1, source_target_pairs={{0,8},{8,16},{16,24},{24,32},{32,40},{40,48},{48,56},{56,64},{64,7... | collective-permute-start | bytes 110600 | tf_op jit(solution)/shard_map/ppermute | solution.py:18
  424.2 5.0 collective-permute-start.1
  429.2 6.4 %collective-permute-start.2 = (bf16[9,2048]{1,0:T(8,128)(2,1)S(1)}, bf16[9,2048]{1,0:T(8,128)(2,1)S(1)}, u32[]{:S(2)}, u32[]{:S(2)}) collective-permute-start(bf16[9,2048]{1,0:T(8,128)(2,1)S(1)} %collective-permute-done), channel_id=1, source_target_pairs={{0,8},{8,16},{16,24},{24,32},{32,40},{40,48},{48,56},{56,64},{64,7... | collective-permute-start | bytes 110600 | tf_op jit(solution)/shard_map/ppermute | solution.py:18
  429.2 6.4 %collective-permute-start.3 = (bf16[9,2048]{1,0:T(8,128)(2,1)S(1)}, bf16[9,2048]{1,0:T(8,128)(2,1)S(1)}, u32[]{:S(2)}, u32[]{:S(2)}) collective-permute-start(bf16[9,2048]{1,0:T(8,128)(2,1)S(1)} %collective-permute-done.1), channel_id=1, source_target_pairs={{0,120},{8,0},{16,8},{24,16},{32,24},{40,32},{48,40},{56,48},{64,5... | collective-permute-start | bytes 110600 | tf_op jit(solution)/shard_map/ppermute | solution.py:21
  435.6 6.4 %collective-permute-start.4 = (bf16[9,2048]{1,0:T(8,128)(2,1)S(1)}, bf16[9,2048]{1,0:T(8,128)(2,1)S(1)}, u32[]{:S(2)}, u32[]{:S(2)}) collective-permute-start(bf16[9,2048]{1,0:T(8,128)(2,1)S(1)} %collective-permute-done.2), channel_id=1, source_target_pairs={{0,8},{8,16},{16,24},{24,32},{32,40},{40,48},{48,56},{56,64},{64,7... | collective-permute-start | bytes 110600 | tf_op jit(solution)/shard_map/ppermute | solution.py:18
  435.6 6.4 %collective-permute-start.5 = (bf16[9,2048]{1,0:T(8,128)(2,1)S(1)}, bf16[9,2048]{1,0:T(8,128)(2,1)}, u32[]{:S(2)}, u32[]{:S(2)}) collective-permute-start(bf16[9,2048]{1,0:T(8,128)(2,1)S(1)} %collective-permute-done.3), channel_id=1, source_target_pairs={{0,120},{8,0},{16,8},{24,16},{32,24},{40,32},{48,40},{56,48},{64,5... | collective-permute-start | bytes 110600 | tf_op jit(solution)/shard_map/ppermute | solution.py:21
  442.1 7.2 %collective-permute-start.6 = (bf16[9,2048]{1,0:T(8,128)(2,1)S(1)}, bf16[9,2048]{1,0:T(8,128)(2,1)}, u32[]{:S(2)}, u32[]{:S(2)}) collective-permute-start(bf16[9,2048]{1,0:T(8,128)(2,1)S(1)} %collective-permute-done.4), channel_id=1, source_target_pairs={{0,8},{8,16},{16,24},{24,32},{32,40},{40,48},{48,56},{56,64},{64,7... | collective-permute-start | bytes 110600 | tf_op jit(solution)/shard_map/ppermute | solution.py:18
  442.1 25.4 %collective-permute-start.7 = (bf16[9,2048]{1,0:T(8,128)(2,1)}, bf16[9,2048]{1,0:T(8,128)(2,1)}, u32[]{:S(2)}, u32[]{:S(2)}) collective-permute-start(bf16[9,2048]{1,0:T(8,128)(2,1)} %collective-permute-done.5), channel_id=1, source_target_pairs={{0,120},{8,0},{16,8},{24,16},{32,24},{40,32},{48,40},{56,48},{64,5... | collective-permute-start | bytes 110600 | tf_op jit(solution)/shard_map/ppermute | solution.py:21
  449.2 23.9 %collective-permute-start.8 = (bf16[9,2048]{1,0:T(8,128)(2,1)}, bf16[9,2048]{1,0:T(8,128)(2,1)}, u32[]{:S(2)}, u32[]{:S(2)}) collective-permute-start(bf16[9,2048]{1,0:T(8,128)(2,1)} %collective-permute-done.6), channel_id=1, source_target_pairs={{0,8},{8,16},{16,24},{24,32},{32,40},{40,48},{48,56},{56,64},{64,7... | collective-permute-start | bytes 110600 | tf_op jit(solution)/shard_map/ppermute | solution.py:18
  453.1 118.1 %all-to-all-start.1 = ((bf16[128,2,1024]{2,1,0:T(2,128)(2,1)}), bf16[128,2,1024]{2,1,0:T(2,128)(2,1)S(1)}, u32[]{:S(2)}, u32[]{:S(2)}) async-start(bf16[128,2,1024]{2,1,0:T(2,128)(2,1)} %reshape.484), calls=%async_computation.3 | async-start | bytes 1048576 | tf_op jit(solution)/shard_map/all_to_all | solution.py:95
  467.5 8.5 %collective-permute-start.9 = (bf16[9,2048]{1,0:T(8,128)(2,1)}, bf16[9,2048]{1,0:T(8,128)(2,1)S(1)}, u32[]{:S(2)}, u32[]{:S(2)}) collective-permute-start(bf16[9,2048]{1,0:T(8,128)(2,1)} %collective-permute-done.7), channel_id=1, source_target_pairs={{0,120},{8,0},{16,8},{24,16},{32,24},{40,32},{48,40},{56,48},{64,5... | collective-permute-start | bytes 110600 | tf_op jit(solution)/shard_map/ppermute | solution.py:21
  473.1 8.7 %collective-permute-start.10 = (bf16[9,2048]{1,0:T(8,128)(2,1)}, bf16[9,2048]{1,0:T(8,128)(2,1)S(1)}, u32[]{:S(2)}, u32[]{:S(2)}) collective-permute-start(bf16[9,2048]{1,0:T(8,128)(2,1)} %collective-permute-done.8), channel_id=1, source_target_pairs={{0,8},{8,16},{16,24},{24,32},{32,40},{40,48},{48,56},{56,64},{64,7... | collective-permute-start | bytes 110600 | tf_op jit(solution)/shard_map/ppermute | solution.py:18
  476.0 6.9 %collective-permute-start.11 = (bf16[9,2048]{1,0:T(8,128)(2,1)S(1)}, bf16[9,2048]{1,0:T(8,128)(2,1)S(1)}, u32[]{:S(2)}, u32[]{:S(2)}) collective-permute-start(bf16[9,2048]{1,0:T(8,128)(2,1)S(1)} %collective-permute-done.9), channel_id=1, source_target_pairs={{0,120},{8,0},{16,8},{24,16},{32,24},{40,32},{48,40},{56,48},{64,5... | collective-permute-start | bytes 110600 | tf_op jit(solution)/shard_map/ppermute | solution.py:21
  481.8 6.4 %collective-permute-start.12 = (bf16[9,2048]{1,0:T(8,128)(2,1)S(1)}, bf16[9,2048]{1,0:T(8,128)(2,1)S(1)}, u32[]{:S(2)}, u32[]{:S(2)}) collective-permute-start(bf16[9,2048]{1,0:T(8,128)(2,1)S(1)} %collective-permute-done.10), channel_id=1, source_target_pairs={{0,8},{8,16},{16,24},{24,32},{32,40},{40,48},{48,56},{56,64},{64,7... | collective-permute-start | bytes 110600 | tf_op jit(solution)/shard_map/ppermute | solution.py:18
  483.0 16.4 %collective-permute-start.13 = (bf16[9,2048]{1,0:T(8,128)(2,1)S(1)}, bf16[9,2048]{1,0:T(8,128)(2,1)S(1)}, u32[]{:S(2)}, u32[]{:S(2)}) collective-permute-start(bf16[9,2048]{1,0:T(8,128)(2,1)S(1)} %collective-permute-done.11), channel_id=1, source_target_pairs={{0,120},{8,0},{16,8},{24,16},{32,24},{40,32},{48,40},{56,48},{64,5... | collective-permute-start | bytes 110600 | tf_op jit(solution)/shard_map/ppermute | solution.py:21
  488.3 11.7 %collective-permute-start.14 = (bf16[9,2048]{1,0:T(8,128)(2,1)S(1)}, bf16[9,2048]{1,0:T(8,128)(2,1)S(1)}, u32[]{:S(2)}, u32[]{:S(2)}) collective-permute-start(bf16[9,2048]{1,0:T(8,128)(2,1)S(1)} %collective-permute-done.12), channel_id=1, source_target_pairs={{0,8},{8,16},{16,24},{24,32},{32,40},{40,48},{48,56},{56,64},{64,7... | collective-permute-start | bytes 110600 | tf_op jit(solution)/shard_map/ppermute | solution.py:18
  (17 other events, 162.1 us)
Sparse Core Ops, SparseCore 0:
  10.8 4.6 sort.21.cloned.1.call-done
  54.8 28.7 all-gather.2
  137.1 51.3 reduce-scatter.2
  191.3 71.0 all-gather.4
  288.0 109.9 reduce-scatter.4
  (1 shorter events, 0.0 us)
